TPU v7x, 512 devices: a whole 4x8x8 slice. The times are simulated.
512 devices in a mesh: blk: 8 (over z_hi, core), win: 64 (over x, y, z_lo).
Axes of the slice: x: 4, y: 8, z: 8 (z_hi: 4, z_lo: 2; z = z_hi * 2 + z_lo), core: 2. Of those that a mesh axis runs over, the one named last changes fastest.
Arguments:
- frame_tokens: bfloat16 [8, 64, 128, 1024], P('blk', 'win'), may hold values from -21 to 21, as said below
- w_kv: bfloat16 [1024, 2048], replicated, may hold values from -0.1875 to 0.1875
- w_q: bfloat16 [1024, 1024], P('win'), may hold values from -0.1875 to 0.1875
- w_out: bfloat16 [1024, 1024], P('win'), may hold values from -0.1875 to 0.1875
- slot_tokens: int32 [8, 64, 128], P(None, 'win'), may hold values from 0 to 1023, as said below
- counts: int32 [8, 64], P('blk', 'win'), may hold values from 32 to 128, as said below
Outputs:
- projected: bfloat16 [8, 64, 128, 1024], P('blk', 'win')
Inputs may be any that keep to these rules, and one draw needn't show every extreme that they name: `frame_tokens`: shown draw: a normal law truncated at 6. `slot_tokens`: every slot names a token of its own window. For each frame group and window the 128 slots name tokens of exactly 4 frames, 32 from each; no token of a window is named twice. `counts`: slots below the count are live. Each window has a frame group with all 128 slots live.
All inputs are finite; a program needn't handle non-finite values.
Results may differ from a plain program's by a relative error of at most 0.012.
The roundings to bfloat16 on the way count: a program that leaves them out, or rounds other values in their place, can miss the bound.
Values may be sent and summed in bfloat16 or wider, within the bound.
A program may use at most 64 MiB of HBM per device.

v0:
```python
import jax
import jax.numpy as jnp
from jax import lax
from jax.sharding import PartitionSpec as P

HEADS = 16


def add_rows(left_rows, shard_rows):
    return jnp.dot(left_rows, shard_rows, preferred_element_type=jnp.float32)


def absorb(state_now, key_rows, value_rows, query_heads, score_scale):
    row_peak, total_sum, accum_rows = state_now
    win_dev, slot_count, head_count, head_dim = query_heads.shape
    key_heads = key_rows.reshape(win_dev, -1, head_count, head_dim)
    value_heads = value_rows.reshape(win_dev, -1, head_count, head_dim)
    scores = (
        jnp.einsum("jshd,jkhd->jhsk", query_heads, key_heads, preferred_element_type=jnp.float32)
        * score_scale
    )
    new_peak = jnp.maximum(row_peak, jnp.max(scores, axis=-1))
    raw_weights = jnp.exp(scores - new_peak[..., None])
    total_sum = jnp.sum(raw_weights, axis=-1)
    mixed_rows = jnp.einsum(
        "jhsk,jkhd->jshd",
        raw_weights.astype(jnp.bfloat16),
        value_heads,
        preferred_element_type=jnp.float32,
    )
    accum_rows = mixed_rows
    return (new_peak, total_sum, accum_rows)


def local(frame_tokens, w_kv, w_q, w_out, slot_tokens, counts):
    groups = lax.axis_size("blk")
    group_at = lax.axis_index("blk")
    frames_here, win_dev, window_len, model_width = frame_tokens.shape
    slot_count = slot_tokens.shape[2]
    per_owner = slot_count // min(4, groups)
    head_count = HEADS
    head_dim = model_width // head_count
    score_scale = head_dim ** (-0.5)
    frame_rows = frame_tokens[0]
    source_group = slot_tokens // window_len
    is_mine = source_group == group_at
    mine_count = is_mine.astype(jnp.int32)
    rank_of = jnp.cumsum(mine_count, axis=-1) - mine_count
    place_at = jnp.where(is_mine, rank_of, per_owner)
    slot_onehot = (place_at[..., None] == jnp.arange(per_owner, dtype=jnp.int32)).astype(
        jnp.bfloat16
    )
    token_onehot = (
        (slot_tokens - group_at * window_len)[..., None] == jnp.arange(window_len, dtype=jnp.int32)
    ).astype(jnp.bfloat16)
    selector = jnp.einsum(
        "gjsc,gjsu->gjcu", slot_onehot, token_onehot, preferred_element_type=jnp.float32
    ).astype(jnp.bfloat16)
    outgoing = jnp.einsum(
        "gjcu,jud->jgcd", selector, frame_rows, preferred_element_type=jnp.float32
    ).astype(jnp.bfloat16)
    arrived = lax.all_to_all(outgoing, "blk", split_axis=1, concat_axis=1, tiled=True)
    incoming = arrived.reshape(win_dev, groups * per_owner, model_width)
    own_picks = lax.dynamic_index_in_dim(slot_tokens, group_at, 0, keepdims=False)
    own_source = own_picks // window_len
    hit_table = (own_source[..., None] == jnp.arange(groups, dtype=jnp.int32)).astype(jnp.int32)
    before = jnp.cumsum(hit_table, axis=1) - hit_table
    order_in = jnp.sum(before * hit_table, axis=-1)
    spot_at = own_source * per_owner + order_in
    grab_rows = (spot_at[..., None] == jnp.arange(groups * per_owner, dtype=jnp.int32)).astype(
        jnp.bfloat16
    )
    picked_rows = (
        jnp.einsum("jsr,jrd->jsd", grab_rows, incoming, preferred_element_type=jnp.float32)
        .astype(jnp.bfloat16)
        .reshape(-1, model_width)
    )
    query_flat = add_rows(picked_rows, lax.all_gather(w_q, "win", axis=0, tiled=True))
    query_heads = query_flat.astype(jnp.bfloat16).reshape(win_dev, slot_count, head_count, head_dim)
    initial = (
        jnp.full((win_dev, head_count, slot_count), -1e30, jnp.float32),
        jnp.zeros((win_dev, head_count, slot_count), jnp.float32),
        jnp.zeros((win_dev, slot_count, head_count, head_dim), jnp.float32),
    )
    key_value = jnp.einsum(
        "fjpd,de->jfpe",
        lax.all_gather(frame_tokens, "blk", axis=0, tiled=True),
        w_kv,
        preferred_element_type=jnp.float32,
    ).astype(jnp.bfloat16)
    key_value = key_value.reshape(win_dev, -1, 2 * model_width)
    state_end = absorb(
        initial,
        key_value[..., :model_width],
        key_value[..., model_width:],
        query_heads,
        score_scale,
    )
    final_peak, final_total, final_accum = state_end
    attended = (
        (final_accum / jnp.transpose(final_total, (0, 2, 1))[..., None])
        .astype(jnp.bfloat16)
        .reshape(-1, model_width)
    )
    out_sum = add_rows(attended, lax.all_gather(w_out, "win", axis=0, tiled=True))
    live_mask = (jnp.arange(slot_count, dtype=jnp.int32)[None, :] < counts[0][:, None]).astype(
        jnp.float32
    )
    return (
        (out_sum * live_mask.reshape(-1, 1))
        .astype(jnp.bfloat16)
        .reshape(1, win_dev, slot_count, model_width)
    )


def solution(mesh):
    placed = (
        P("blk", "win", None, None),
        P(),
        P("win", None),
        P("win", None),
        P(None, "win", None),
        P("blk", "win"),
    )
    return jax.shard_map(
        local, mesh=mesh, in_specs=placed, out_specs=P("blk", "win", None, None), check_vma=False
    )
```

profile of v0, /device:TPU:8, one launch (start us, length us, event | category | flops | bytes accessed | tf_op | source)
XLA Modules:
  0.0 670.5 jit_solution(2670747314636077683)
XLA Ops:
  6.5 0.7 all-gather.4.cloned.1.call-update
  7.3 0.7 all-gather.6.cloned.1.call-update
  8.0 0.7 fusion.39
  8.7 0.3 reduce_window_sum.23
  9.0 0.7 broadcast_subtract_fusion
  9.7 2.3 fusion.15
  12.0 10.3 %all-to-all-start = ((bf16[1,8,32,1024]{3,2,0,1:T(8,128)(2,1)}), bf16[1,8,32,1024]{3,2,0,1:T(8,128)(2,1)S(1)}, u32[]{:S(2)}, u32[]{:S(2)}) async-start(bf16[1,8,32,1024]{3,2,0,1:T(8,128)(2,1)} %fusion.15), calls=%async_computation | async-start | bytes 1048576 | tf_op jit(solution)/shard_map/all_to_all | solution.py:62
  22.3 0.7 all-gather.8.cloned.1.call-update
  23.0 0.7 and_select_fusion
  23.8 0.2 reduce_window_sum.22
  24.6 0.2 select_reduce_fusion
  24.8 0.7 multiply_add_fusion
  25.5 30.7 %all-gather.4.cloned.1.call-done = bf16[8,1,128,1024]{3,2,1,0:T(8,128)(2,1)} async-done(((bf16[1,1,128,1024]{3,2,1,0:T(8,128)(2,1)}), bf16[8,1,128,1024]{3,2,1,0:T(8,128)(2,1)}) %all-gather.4.cloned.1.call-update) | async-done | bytes 2097168 | tf_op jit(solution)/shard_map/all_gather | solution.py:87
  56.2 7.4 %fusion.8 = bf16[2048,8,128]{0,2,1:T(8,128)(2,1)S(1)} fusion(bf16[1024,2048]{1,0:T(8,128)(2,1)} %param.7, bf16[8,1,128,1024]{3,2,1,0:T(8,128)(2,1)} %all-gather.4.cloned.1.call-done), kind=kOutput, calls=%fused_computation.9 | convolution fusion | flops 4297064448 | bytes 10485760 | tf_op jit(solution)/shard_map/fjpd,de->jfpe/dot_general | solution.py:85
  63.6 1.8 fusion.41
  65.4 2.6 copy.23
  67.9 2.9 copy.30
  70.8 289.0 %all-gather.6.cloned.1.call-done = bf16[1024,1024]{1,0:T(8,128)(2,1)} async-done(((bf16[16,1024]{1,0:T(8,128)(2,1)}), bf16[1024,1024]{1,0:T(8,128)(2,1)}) %all-gather.6.cloned.1.call-update) | async-done | bytes 2097168 | tf_op jit(solution)/shard_map/all_gather | solution.py:78
  359.8 2.2 convolution_convert_fusion.1
  362.2 1.4 multiply_reduce_fusion
  363.6 1.8 fusion
  365.5 2.0 fusion.21
  367.5 293.7 %all-gather.8.cloned.1.call-done = bf16[1024,1024]{1,0:T(8,128)(2,1)} async-done(((bf16[16,1024]{1,0:T(8,128)(2,1)}), bf16[1024,1024]{1,0:T(8,128)(2,1)}) %all-gather.8.cloned.1.call-update) | async-done | bytes 2097168 | tf_op jit(solution)/shard_map/all_gather | solution.py:105
  661.2 2.8 fusion.17
  (11 shorter events, 0.3 us)
Async XLA Ops:
  6.5 49.7 %all-gather.4.cloned.1.call-start = ((), (), s32[]{:S(2)}) async-start(), calls=%async_computation.1 | async-start | bytes 2359296 | tf_op jit(solution)/shard_map/all_gather | solution.py:87
  7.3 352.6 %all-gather.6.cloned.1.call-start = ((), (), s32[]{:S(2)}) async-start(), calls=%async_computation.2 | async-start | bytes 2129920 | tf_op jit(solution)/shard_map/all_gather | solution.py:78
  12.0 58.8 %all-to-all-start = ((bf16[1,8,32,1024]{3,2,0,1:T(8,128)(2,1)}), bf16[1,8,32,1024]{3,2,0,1:T(8,128)(2,1)S(1)}, u32[]{:S(2)}, u32[]{:S(2)}) async-start(bf16[1,8,32,1024]{3,2,0,1:T(8,128)(2,1)} %fusion.15), calls=%async_computation | async-start | bytes 1048576 | tf_op jit(solution)/shard_map/all_to_all | solution.py:62
  22.3 638.9 %all-gather.8.cloned.1.call-start = ((), (), s32[]{:S(2)}) async-start(), calls=%async_computation.3 | async-start | bytes 2129920 | tf_op jit(solution)/shard_map/all_gather | solution.py:105
  363.6 1.8 copy-start
Sparse Core Ops, SparseCore 0:
  9.5 46.6 all-gather.3
  58.3 301.5 all-gather.5
  361.9 299.2 all-gather.7
where the time goes:
time: 671 us; the launch traced here: 670 us
  waiting for transfers between devices  616 us (92%)
  matrix products  18.1 us (3%)
  between operations  13.9 us (2%)
  starting transfers between devices  10.4 us (2%)
  local copies, waits for them, and re-layouts  7.37 us (1%)
    all_gather x1, waiting for transfers between devices, local(): lax.all_gather(w_out, 'win', axis=0, tiled=True)  294 us
    all_gather x1, waiting for transfers between devices, local(): lax.all_gather(w_q, 'win', axis=0, tiled=True)  289 us
    all_gather x1, waiting for transfers between devices, local(): lax.all_gather(frame_tokens, 'blk', axis=0, tiled=True)  30.7 us
  transfers between devices with their start and end apart: 4, of which 3 were waited for; matrix products, arithmetic and copies ran while one was open for 4% of the time, Pallas kernels for 0%

commit v1 on v0

v1 whole, which is shorter than its diff:
```python
import functools

import jax
import jax.numpy as jnp
from jax import lax
from jax.experimental import pallas as pl
from jax.experimental.pallas import tpu as pltpu
from jax.sharding import PartitionSpec as P

HEADS = 16
NX, NY, NZ = 4, 8, 4
MESH = pl.DeviceIdType.MESH
F32 = jnp.float32
BF16 = jnp.bfloat16

NAMES = ["tp0", "tp1", "tm0", "tm1", "tf0", "tf1", "ts1", "ts4", "ts5", "ts70", "ts71"]
for _i in range(2):
    NAMES += [f"pair{_i}"]
    NAMES += [f"yo{_i}{_d}" for _d in range(1, NY)] + [f"yp{_i}{_d}" for _d in range(1, NY)]
    NAMES += [f"x{_k}{_i}" for _k in ("p0", "p1", "m0", "m1", "f0", "f1", "s0", "sm", "sp", "so")]
INDEX = {name: at for at, name in enumerate(NAMES)}


def kernel(tok_in, wkv_in, wq_in, wo_in, slots_ref, counts_ref, out_ref,
           tok, wkv, wq, wo, kv, qs, att, picked, send, recv, near):
    b = lax.axis_index("blk")
    w = lax.axis_index("win")
    core, zh = lax.rem(b, 2), b // 2
    zl, y, x = lax.rem(w, 2), lax.rem(w // 2, NY), w // (2 * NY)

    def at_blk(z, c):
        return (lax.rem(z + NZ, NZ) * 2 + c, w)

    def at_win(xx, yy, zz):
        return (b, (lax.rem(xx + NX, NX) * NY + lax.rem(yy, NY)) * 2 + zz)

    sib = (b + 1 - 2 * core, w)
    zp, zm = at_blk(zh + 1, core), at_blk(zh - 1, core)
    pair = at_win(x, y, 1 - zl)
    xp, xm = at_win(x + 1, y, zl), at_win(x - 1, y, zl)
    peers = [at_win(x, y + d, zl) for d in range(1, NY)]

    started = []

    def move(name, src, dst, device):
        copy = pltpu.make_async_remote_copy(
            src_ref=src, dst_ref=dst, send_sem=send.at[INDEX[name]], recv_sem=recv.at[INDEX[name]],
            device_id=device, device_id_type=MESH,
        )
        copy.start()
        started.append(copy)

    def got(name, dst):
        pltpu.make_async_remote_copy(
            src_ref=dst, dst_ref=dst, send_sem=send.at[INDEX[name]], recv_sem=recv.at[INDEX[name]],
            device_id=sib, device_id_type=MESH,
        ).wait_recv()

    barrier = pltpu.get_barrier_semaphore()
    everyone = [sib, zp, zm, pair, xp, xm] + peers
    for device in everyone:
        pl.semaphore_signal(barrier, inc=1, device_id=device, device_id_type=MESH)
    load_tok = pltpu.make_async_copy(tok_in.at[0, 0], tok.at[0], near.at[0])
    load_tok.start()
    load_kv = pltpu.make_async_copy(wkv_in, wkv, near.at[1])
    load_kv.start()
    cols = pl.ds(pl.multiple_of(core * 512, 512), 512)
    mine = pl.ds(pl.multiple_of(y * 32 + zl * 16, 16), 16)
    other = pl.ds(pl.multiple_of(y * 32 + (1 - zl) * 16, 16), 16)
    weights = ((0, wq_in, wq), (1, wo_in, wo))
    loads = []
    for i, src, buf in weights:
        copy = pltpu.make_async_copy(src.at[:, cols], buf.at[x, mine, cols], near.at[2 + i])
        copy.start()
        loads.append(copy)
    pl.semaphore_wait(barrier, len(everyone))

    def half(h):
        return pl.ds(64 * h, 64)

    def upper(h):
        return pl.ds(128 * h, 128)

    for i, src, buf in weights:
        move(f"pair{i}", src.at[:, cols], buf.at[x, mine, cols], pair)
    move("tp0", tok_in.at[0, 0, half(0)], tok.at[2, half(0)], zp)
    move("tm1", tok_in.at[0, 0, half(1)], tok.at[3, half(1)], zm)
    move("tp1", tok_in.at[0, 0, half(1)], tok.at[2, half(1)], zp)
    move("tm0", tok_in.at[0, 0, half(0)], tok.at[3, half(0)], zm)
    move("ts1", tok_in.at[0, 0], tok.at[1], sib)
    for i, src, buf in weights:
        for d in range(1, NY):
            move(f"yo{i}{d}", src.at[:, cols], buf.at[x, mine, cols], peers[d - 1])
        if i == 0:
            for k, _, buf2 in weights:
                got(f"pair{k}", buf2.at[x, other, cols])
        for d in range(1, NY):
            move(f"yp{i}{d}", buf.at[x, other, cols], buf.at[x, other, cols], peers[d - 1])

    def slab(buf, k, h=None):
        if h is None:
            return buf.at[lax.rem(x + k + NX, NX), :, cols]
        return buf.at[lax.rem(x + k + NX, NX), upper(h), cols]

    def wait_y(i, buf):
        loads[i].wait()
        for d in range(1, NY):
            yy = lax.rem(y + NY - d, NY)
            got(f"yo{i}{d}", buf.at[x, pl.ds(pl.multiple_of(yy * 32 + zl * 16, 16), 16), cols])
            got(f"yp{i}{d}", buf.at[x, pl.ds(pl.multiple_of(yy * 32 + (1 - zl) * 16, 16), 16), cols])
        move(f"xp0{i}", slab(buf, 0, 0), slab(buf, 0, 0), xp)
        move(f"xm1{i}", slab(buf, 0, 1), slab(buf, 0, 1), xm)
        move(f"xp1{i}", slab(buf, 0, 1), slab(buf, 0, 1), xp)
        move(f"xm0{i}", slab(buf, 0, 0), slab(buf, 0, 0), xm)
        move(f"xs0{i}", slab(buf, 0), slab(buf, 0), sib)

    def wait_x1(i, buf):
        got(f"xp0{i}", slab(buf, -1, 0))
        move(f"xf0{i}", slab(buf, -1, 0), slab(buf, -1, 0), xp)
        got(f"xm1{i}", slab(buf, 1, 1))
        move(f"xf1{i}", slab(buf, 1, 1), slab(buf, 1, 1), xm)

    def wait_x2(i, buf):
        got(f"xp1{i}", slab(buf, -1, 1))
        move(f"xsm{i}", slab(buf, -1), slab(buf, -1), sib)
        got(f"xm0{i}", slab(buf, 1, 0))
        move(f"xsp{i}", slab(buf, 1), slab(buf, 1), sib)

    def wait_x3(i, buf):
        got(f"xf0{i}", slab(buf, 2, 0))
        got(f"xf1{i}", slab(buf, 2, 1))
        move(f"xso{i}", slab(buf, 2), slab(buf, 2), sib)

    other_cols = pl.ds(pl.multiple_of((1 - core) * 512, 512), 512)

    def wait_s(i, buf):
        for k, name in ((0, "xs0"), (-1, "xsm"), (1, "xsp"), (2, "xso")):
            got(f"{name}{i}", buf.at[lax.rem(x + k + NX, NX), :, other_cols])

    def make_kv(j):
        rows = tok[pl.ds(j, 2)].reshape(256, 1024)

        @pl.loop(0, 4)
        def _(n):
            at = pl.ds(pl.multiple_of(n * 512, 512), 512)
            kv[pl.ds(128 * j, 256), at] = jnp.dot(rows, wkv[:, at], preferred_element_type=F32).astype(BF16)

    frames = [b, b + 1 - 2 * core, zm[0], zp[0], zm[0] + 1 - 2 * core, zp[0] + 1 - 2 * core]
    opposite = lax.rem(zh + 2, NZ) * 2 + core
    frames += [opposite, opposite + 1 - 2 * core]
    wanted = slots_ref[pl.ds(b, 1), 0, :]

    def pick(j):
        hits = []
        for k in (j, j + 1):
            token = lax.broadcasted_iota(jnp.int32, (128, 128), 0) + frames[k] * 128
            hits.append(jnp.where(token == wanted, 1.0, 0.0).T.astype(BF16))
        rows = tok[pl.ds(j, 2)].reshape(256, 1024)
        part = jnp.dot(jnp.concatenate(hits, axis=1), rows, preferred_element_type=F32)
        if j == 0:
            picked[...] = part
        else:
            picked[...] += part

    load_tok.wait()
    load_kv.wait()
    got("ts1", tok.at[1])
    make_kv(0)
    pick(0)
    got("tp0", tok.at[2, half(0)])
    move("tf0", tok.at[2, half(0)], tok.at[6, half(0)], zp)
    got("tm1", tok.at[3, half(1)])
    move("tf1", tok.at[3, half(1)], tok.at[6, half(1)], zm)
    wait_y(0, wq)
    got("tp1", tok.at[2, half(1)])
    move("ts4", tok.at[2], tok.at[4], sib)
    got("tm0", tok.at[3, half(0)])
    move("ts5", tok.at[3], tok.at[5], sib)
    wait_y(1, wo)
    make_kv(2)
    pick(2)
    wait_x1(0, wq)
    got("ts4", tok.at[4])
    got("ts5", tok.at[5])
    make_kv(4)
    pick(4)
    wait_x2(0, wq)
    wait_x1(1, wo)
    got("tf0", tok.at[6, half(0)])
    move("ts70", tok.at[6, half(0)], tok.at[7, half(0)], sib)
    got("tf1", tok.at[6, half(1)])
    move("ts71", tok.at[6, half(1)], tok.at[7, half(1)], sib)
    wait_x3(0, wq)
    got("ts70", tok.at[7, half(0)])
    got("ts71", tok.at[7, half(1)])
    make_kv(6)
    pick(6)
    wait_x2(1, wo)
    wait_s(0, wq)
    qs[...] = jnp.dot(picked[...].astype(BF16), wq[...].reshape(1024, 1024), preferred_element_type=F32).astype(BF16)
    wait_x3(1, wo)

    scale = 64 ** -0.5 * 1.4426950408889634
    lane = lax.broadcasted_iota(jnp.int32, (128, 128), 1)

    @pl.loop(0, HEADS // 2)
    def _(n):
        at = pl.ds(pl.multiple_of(n * 128, 128), 128)
        rows = qs[:, at]
        zero = jnp.zeros_like(rows)
        both = jnp.concatenate([jnp.where(lane < 64, rows, zero), jnp.where(lane >= 64, rows, zero)], axis=0)
        scores = lax.dot_general(both, kv[:, at], (((1,), (1,)), ((), ())), preferred_element_type=F32)
        peak = jnp.max(scores, axis=-1, keepdims=True)
        raw = jnp.exp2((scores - peak) * scale)
        total = jnp.sum(raw, axis=-1, keepdims=True)
        values = kv[:, pl.ds(pl.multiple_of(n * 128 + 1024, 128), 128)]
        mixed = jnp.dot(raw.astype(BF16), values, preferred_element_type=F32) / total
        att[:, at] = jnp.where(lane < 64, mixed[:128], mixed[128:]).astype(BF16)

    wait_s(1, wo)
    live = lax.broadcasted_iota(jnp.int32, (128, 1024), 0) < counts_ref[0, 0]
    result = jnp.dot(att[...], wo[...].reshape(1024, 1024), preferred_element_type=F32)
    out_ref[0, 0] = (result * jnp.where(live, 1.0, 0.0)).astype(BF16)
    for copy in started:
        copy.wait_send()


def local(frame_tokens, w_kv, w_q, w_out, slot_tokens, counts):
    hbm = pl.BlockSpec(memory_space=pl.ANY)
    vmem = pl.BlockSpec(memory_space=pltpu.VMEM)
    return pl.pallas_call(
        kernel,
        out_shape=jax.ShapeDtypeStruct((1, 1, 128, 1024), BF16),
        in_specs=[hbm, hbm, hbm, hbm, vmem, pl.BlockSpec(memory_space=pltpu.SMEM)],
        out_specs=vmem,
        scratch_shapes=[
            pltpu.VMEM((8, 128, 1024), BF16),
            pltpu.VMEM((1024, 2048), BF16),
            pltpu.VMEM((NX, 256, 1024), BF16),
            pltpu.VMEM((NX, 256, 1024), BF16),
            pltpu.VMEM((1024, 2048), BF16),
            pltpu.VMEM((128, 1024), BF16),
            pltpu.VMEM((128, 1024), BF16),
            pltpu.VMEM((128, 1024), F32),
            pltpu.SemaphoreType.DMA((len(NAMES),)),
            pltpu.SemaphoreType.DMA((len(NAMES),)),
            pltpu.SemaphoreType.DMA((4,)),
        ],
        compiler_params=pltpu.CompilerParams(
            collective_id=0, has_side_effects=True, vmem_limit_bytes=56 * 1024 * 1024
        ),
    )(frame_tokens, w_kv, w_q, w_out, slot_tokens, counts)


def solution(mesh):
    placed = (
        P("blk", "win", None, None),
        P(),
        P("win", None),
        P("win", None),
        P(None, "win", None),
        P("blk", "win"),
    )
    return jax.shard_map(
        local, mesh=mesh, in_specs=placed, out_specs=P("blk", "win", None, None), check_vma=False
    )
```

time: 671 us -> 57.4 us (0.09)
  the two profiles are of different devices: /device:TPU:8 before, /device:TPU:1 now
where the time goes in v1:
time: 57.4 us; the launch traced here: 57.2 us
  Pallas kernels  54.9 us (96%)
  local copies, waits for them, and re-layouts  1.67 us (3%)
  between operations  0.66 us (1%)
    pallas_call x1, Pallas kernels, local(): pl.pallas_call(kernel, out_shape=jax.ShapeDtypeStruct((1, 1, 128, 1024),...  54.9 us
    unnamed x1, local copies, waits for them, and re-layouts  1.67 us

profile of v1, /device:TPU:1, one launch (start us, length us, event | category | flops | bytes accessed | tf_op | source)
XLA Modules:
  0.0 57.2 jit_solution(2575548732257166397)
XLA Ops:
  0.7 54.9 %shard_map.64 = bf16[1,1,128,1024]{3,2,1,0:T(8,128)(2,1)} custom-call(bf16[1,1,128,1024]{3,2,1,0:T(8,128)(2,1)} %tok_in.1, bf16[1024,2048]{1,0:T(8,128)(2,1)} %wkv_in.1, bf16[16,1024]{1,0:T(8,128)(2,1)} %wq_in.1, bf16[16,1024]{1,0:T(8,128)(2,1)} %wo_in.1, s32[8,1,128]{2,1,0:T(1,128)} %slots_ref.1, s32[1,1]{1,0:T(1,128)S(6)} %copy.8.counts_ref), custom_call_target="tpu_custom_call" | custom-call | tf_op jit(solution)/shard_map/pallas_call | solution.py:231
  55.5 1.7 %copy.9 = bf16[1,1,128,1024]{3,2,1,0:T(8,128)(2,1)} copy(bf16[1,1,128,1024]{3,2,1,0:T(8,128)(2,1)} %shard_map.64) | data formatting | bytes 524288

commit v2 on v1

v2 whole, which is shorter than its diff:
```python
import functools

import jax
import jax.numpy as jnp
from jax import lax
from jax.experimental import pallas as pl
from jax.experimental.pallas import tpu as pltpu
from jax.sharding import PartitionSpec as P

HEADS = 16
NX, NY, NZ = 4, 8, 4
MESH = pl.DeviceIdType.MESH
F32 = jnp.float32
BF16 = jnp.bfloat16

NAMES = ["own0", "own1"]
NAMES += [f"z{_k}{_s}{_h}" for _k in "pmf" for _s in range(2) for _h in range(2)]
NAMES += [f"share{_s}" for _s in range(2, 8)]
for _i in range(2):
    NAMES += [f"{_k}{_i}" for _k in ("pair", "y1p", "y1m", "y2p", "y2m", "y3p", "y3m", "y4p", "y4m")]
    NAMES += [f"x{_k}{_i}{_d}" for _k in "pmf" for _d in range(NY)]
    NAMES += [f"slab{_i}{_k}" for _k in range(NX)]
INDEX = {name: at for at, name in enumerate(NAMES)}


def kernel(tok_in, wkv_in, wq_in, wo_in, slots_ref, counts_ref, out_ref,
           tok, wkv, wq, wo, kv, qs, att, picked, send, recv, near):
    b = lax.axis_index("blk")
    w = lax.axis_index("win")
    core, zh = lax.rem(b, 2), b // 2
    zl, y, x = lax.rem(w, 2), lax.rem(w // 2, NY), w // (2 * NY)

    def at_z(d):
        return (lax.rem(zh + d, NZ) * 2, w)

    def at_xy(dx, dy, zz):
        return (b, (lax.rem(x + dx, NX) * NY + lax.rem(y + dy, NY)) * 2 + zz)

    sib = (b + 1 - 2 * core, w)
    zp, zm = at_z(1), at_z(NZ - 1)
    pair = at_xy(0, 0, 1 - zl)
    xp, xm = at_xy(1, 0, zl), at_xy(NX - 1, 0, zl)
    y1p, y1m = at_xy(0, 1, zl), at_xy(0, NY - 1, zl)
    y2p, y2m = at_xy(0, 2, zl), at_xy(0, NY - 2, zl)

    started = {0: [], 1: []}

    def descriptor(name, src, dst, device):
        return pltpu.make_async_remote_copy(
            src_ref=src, dst_ref=dst, send_sem=send.at[INDEX[name]], recv_sem=recv.at[INDEX[name]],
            device_id=device, device_id_type=MESH,
        )

    def move(who, name, src, dst, device):
        descriptor(name, src, dst, device).start()
        size = 1
        for n in dst.shape:
            size *= n
        started[who].append((name, size // 1024))

    def got(name, dst):
        descriptor(name, dst, dst, sib).wait_recv()

    def enter(devices):
        barrier = pltpu.get_barrier_semaphore()
        for device in devices:
            pl.semaphore_signal(barrier, inc=1, device_id=device, device_id_type=MESH)
        pl.semaphore_wait(barrier, len(devices))

    def sent(who):
        for name, rows in started[who]:
            part = tok.at[0, pl.ds(0, rows)] if rows <= 128 else wq.at[0, pl.ds(0, rows)]
            descriptor(name, part, part, sib).wait_send()

    load_tok = pltpu.make_async_copy(tok_in.at[0, 0], tok.at[core], near.at[0])
    load_tok.start()
    load_kv = pltpu.make_async_copy(wkv_in, wkv, near.at[1])
    load_kv.start()

    def make_kv(j):
        rows = tok[pl.ds(j, 2)].reshape(256, 1024)

        @pl.loop(0, 4)
        def _(n):
            at = pl.ds(pl.multiple_of(n * 512, 512), 512)
            kv[pl.ds(128 * j, 256), at] = jnp.dot(rows, wkv[:, at], preferred_element_type=F32).astype(BF16)

    before, after, across = lax.rem(zh + NZ - 1, NZ) * 2, lax.rem(zh + 1, NZ) * 2, lax.rem(zh + 2, NZ) * 2
    frames = [2 * zh, 2 * zh + 1, before, after, before + 1, after + 1, across, across + 1]
    wanted = slots_ref[pl.ds(b, 1), 0, :]

    def pick(j):
        hits = []
        for k in (j, j + 1):
            token = lax.broadcasted_iota(jnp.int32, (128, 128), 0) + frames[k] * 128
            hits.append(jnp.where(token == wanted, 1.0, 0.0).T.astype(BF16))
        rows = tok[pl.ds(j, 2)].reshape(256, 1024)
        part = jnp.dot(jnp.concatenate(hits, axis=1), rows, preferred_element_type=F32)
        if j == 0:
            picked[...] = part
        else:
            picked[...] += part

    def absorb(j):
        make_kv(j)
        pick(j)

    @pl.when(core == 0)
    def _():
        enter([sib, zp, zm])

        def part(slot, h):
            return tok.at[slot, pl.ds(64 * h, 64)]

        def spread(s):
            for k, h in (("p", 0), ("m", 1), ("p", 1), ("m", 0)):
                src = tok_in.at[0, 0, pl.ds(64 * h, 64)] if s == 0 else part(1, h)
                move(0, f"z{k}{s}{h}", src, part((2 if k == "p" else 3) + 2 * s, h), zp if k == "p" else zm)

        def receive(s):
            low, high = 2 + 2 * s, 3 + 2 * s
            got(f"zp{s}0", part(low, 0))
            move(0, f"zf{s}0", part(low, 0), part(6 + s, 0), zp)
            got(f"zm{s}1", part(high, 1))
            move(0, f"zf{s}1", part(high, 1), part(6 + s, 1), zm)
            got(f"zp{s}1", part(low, 1))
            move(0, f"share{low}", tok.at[low], tok.at[low], sib)
            got(f"zm{s}0", part(high, 0))
            move(0, f"share{high}", tok.at[high], tok.at[high], sib)

        spread(0)
        move(0, "own0", tok_in.at[0, 0], tok.at[0], sib)
        got("own1", tok.at[1])
        spread(1)
        load_tok.wait()
        load_kv.wait()
        absorb(0)
        receive(0)
        absorb(2)
        receive(1)
        absorb(4)
        for s in range(2):
            got(f"zf{s}0", part(6 + s, 0))
            got(f"zf{s}1", part(6 + s, 1))
            move(0, f"share{6 + s}", tok.at[6 + s], tok.at[6 + s], sib)
        absorb(6)
        for k in range(NX):
            got(f"slab0{k}", wq.at[lax.rem(x + k, NX)])

    def block(buf, k, dx=0, h=None):
        at = lax.rem(y + NY - k, NY) * 32
        if h is None:
            rows = pl.ds(pl.multiple_of(at, 32), 32)
        else:
            rows = pl.ds(pl.multiple_of(at + 16 * h, 16), 16)
        return buf.at[lax.rem(x + dx, NX), rows]

    def slab(i, buf, k):
        whole = buf.at[lax.rem(x + k, NX)]
        move(1, f"slab{i}{k}", whole, whole, sib)

    def over_x(i, buf, k):
        for name, device in (("xp", xp), ("xm", xm)):
            move(1, f"{name}{i}{k}", block(buf, k), block(buf, k), device)

    def pass_x(i, buf, k):
        got(f"xp{i}{k}", block(buf, k, NX - 1))
        if k < 4:
            move(1, f"xf{i}{k}", block(buf, k, NX - 1), block(buf, k, NX - 1), xp)
        got(f"xm{i}{k}", block(buf, k, 1))
        if k >= 4:
            move(1, f"xf{i}{k}", block(buf, k, 1), block(buf, k, 1), xm)

    def last_x(i, buf):
        for k in range(NY):
            got(f"xf{i}{k}", block(buf, k, 2))
        slab(i, buf, 2)

    both = ((0, wq), (1, wo))

    @pl.when(core == 1)
    def _():
        loads = []
        for i, src, buf in ((0, wq_in, wq), (1, wo_in, wo)):
            copy = pltpu.make_async_copy(src, block(buf, 0, 0, zl), near.at[2 + i])
            copy.start()
            loads.append(copy)
        enter([sib, pair, xp, xm, y1p, y1m, y2p, y2m])
        move(1, "pair0", wq_in, block(wq, 0, 0, zl), pair)
        move(1, "pair1", wo_in, block(wo, 0, 0, zl), pair)
        move(1, "own1", tok_in.at[0, 0], tok.at[1], sib)
        for i, buf in both:
            loads[i].wait()
            got(f"pair{i}", block(buf, 0, 0, 1 - zl))
            for name, device in (("y1p", y1p), ("y1m", y1m), ("y2p", y2p), ("y2m", y2m)):
                move(1, f"{name}{i}", block(buf, 0), block(buf, 0), device)
            over_x(i, buf, 0)
        load_tok.wait()
        load_kv.wait()
        got("own0", tok.at[0])
        absorb(0)
        for i, buf in both:
            got(f"y1p{i}", block(buf, 1))
            move(1, f"y3p{i}", block(buf, 1), block(buf, 1), y2p)
            got(f"y1m{i}", block(buf, 7))
            move(1, f"y3m{i}", block(buf, 7), block(buf, 7), y2m)
            got(f"y2p{i}", block(buf, 2))
            move(1, f"y4p{i}", block(buf, 2, 0, 0), block(buf, 2, 0, 0), y2p)
            got(f"y2m{i}", block(buf, 6))
            move(1, f"y4m{i}", block(buf, 6, 0, 1), block(buf, 6, 0, 1), y2m)
        for i, buf in both:
            for k in (1, 7, 2, 6):
                over_x(i, buf, k)
        for i, buf in both:
            pass_x(i, buf, 0)
        got("share2", tok.at[2])
        got("share3", tok.at[3])
        absorb(2)
        for i, buf in both:
            got(f"y3p{i}", block(buf, 3))
            got(f"y3m{i}", block(buf, 5))
            got(f"y4p{i}", block(buf, 4, 0, 0))
            got(f"y4m{i}", block(buf, 4, 0, 1))
            for k in (3, 5, 4):
                over_x(i, buf, k)
            slab(i, buf, 0)
        for i, buf in both:
            for k in (1, 7, 2, 6):
                pass_x(i, buf, k)
        got("share4", tok.at[4])
        got("share5", tok.at[5])
        absorb(4)
        for i, buf in both:
            for k in (3, 5, 4):
                pass_x(i, buf, k)
            slab(i, buf, 3)
            slab(i, buf, 1)
        last_x(0, wq)
        got("share6", tok.at[6])
        got("share7", tok.at[7])
        absorb(6)

    qs[...] = jnp.dot(picked[...].astype(BF16), wq[...].reshape(1024, 1024), preferred_element_type=F32).astype(BF16)

    @pl.when(core == 1)
    def _():
        last_x(1, wo)

    scale = 64 ** -0.5 * 1.4426950408889634
    lane = lax.broadcasted_iota(jnp.int32, (128, 128), 1)

    @pl.loop(0, HEADS // 2)
    def _(n):
        at = pl.ds(pl.multiple_of(n * 128, 128), 128)
        rows = qs[:, at]
        zero = jnp.zeros_like(rows)
        both = jnp.concatenate([jnp.where(lane < 64, rows, zero), jnp.where(lane >= 64, rows, zero)], axis=0)
        scores = lax.dot_general(both, kv[:, at], (((1,), (1,)), ((), ())), preferred_element_type=F32)
        peak = jnp.max(scores, axis=-1, keepdims=True)
        raw = jnp.exp2((scores - peak) * scale)
        total = jnp.sum(raw, axis=-1, keepdims=True)
        values = kv[:, pl.ds(pl.multiple_of(n * 128 + 1024, 128), 128)]
        mixed = jnp.dot(raw.astype(BF16), values, preferred_element_type=F32) / total
        att[:, at] = jnp.where(lane < 64, mixed[:128], mixed[128:]).astype(BF16)

    @pl.when(core == 0)
    def _():
        for k in range(NX):
            got(f"slab1{k}", wo.at[lax.rem(x + k, NX)])

    live = lax.broadcasted_iota(jnp.int32, (128, 1024), 0) < counts_ref[0, 0]
    result = jnp.dot(att[...], wo[...].reshape(1024, 1024), preferred_element_type=F32)
    out_ref[0, 0] = (result * jnp.where(live, 1.0, 0.0)).astype(BF16)

    for who in range(2):
        pl.when(core == who)(functools.partial(sent, who))


def local(frame_tokens, w_kv, w_q, w_out, slot_tokens, counts):
    hbm = pl.BlockSpec(memory_space=pl.ANY)
    vmem = pl.BlockSpec(memory_space=pltpu.VMEM)
    return pl.pallas_call(
        kernel,
        out_shape=jax.ShapeDtypeStruct((1, 1, 128, 1024), BF16),
        in_specs=[hbm, hbm, hbm, hbm, vmem, pl.BlockSpec(memory_space=pltpu.SMEM)],
        out_specs=vmem,
        scratch_shapes=[
            pltpu.VMEM((8, 128, 1024), BF16),
            pltpu.VMEM((1024, 2048), BF16),
            pltpu.VMEM((NX, 256, 1024), BF16),
            pltpu.VMEM((NX, 256, 1024), BF16),
            pltpu.VMEM((1024, 2048), BF16),
            pltpu.VMEM((128, 1024), BF16),
            pltpu.VMEM((128, 1024), BF16),
            pltpu.VMEM((128, 1024), F32),
            pltpu.SemaphoreType.DMA((len(NAMES),)),
            pltpu.SemaphoreType.DMA((len(NAMES),)),
            pltpu.SemaphoreType.DMA((4,)),
        ],
        compiler_params=pltpu.CompilerParams(
            collective_id=0, has_side_effects=True, vmem_limit_bytes=56 * 1024 * 1024
        ),
    )(frame_tokens, w_kv, w_q, w_out, slot_tokens, counts)


def solution(mesh):
    placed = (
        P("blk", "win", None, None),
        P(),
        P("win", None),
        P("win", None),
        P(None, "win", None),
        P("blk", "win"),
    )
    return jax.shard_map(
        local, mesh=mesh, in_specs=placed, out_specs=P("blk", "win", None, None), check_vma=False
    )
```

time: 57.4 us -> 50.5 us (0.88)
  the two profiles are of different devices: /device:TPU:1 before, /device:TPU:73 now
where the time goes in v2:
time: 50.5 us; the launch traced here: 50.3 us
  Pallas kernels  48 us (95%)
  local copies, waits for them, and re-layouts  1.67 us (3%)
  between operations  0.66 us (1%)
    pallas_call x1, Pallas kernels, local(): pl.pallas_call(kernel, out_shape=jax.ShapeDtypeStruct((1, 1, 128, 1024),...  48 us
    unnamed x1, local copies, waits for them, and re-layouts  1.67 us

profile of v2, /device:TPU:73, one launch (start us, length us, event | category | flops | bytes accessed | tf_op | source)
XLA Modules:
  0.0 50.3 jit_solution(9002817550990432653)
XLA Ops:
  0.7 48.0 %shard_map.64 = bf16[1,1,128,1024]{3,2,1,0:T(8,128)(2,1)} custom-call(bf16[1,1,128,1024]{3,2,1,0:T(8,128)(2,1)} %tok_in.1, bf16[1024,2048]{1,0:T(8,128)(2,1)} %wkv_in.1, bf16[16,1024]{1,0:T(8,128)(2,1)} %wq_in.1, bf16[16,1024]{1,0:T(8,128)(2,1)} %wo_in.1, s32[8,1,128]{2,1,0:T(1,128)} %slots_ref.1, s32[1,1]{1,0:T(1,128)S(6)} %copy.8.counts_ref), custom_call_target="tpu_custom_call" | custom-call | tf_op jit(solution)/shard_map/pallas_call | solution.py:282
  48.6 1.7 %copy.9 = bf16[1,1,128,1024]{3,2,1,0:T(8,128)(2,1)} copy(bf16[1,1,128,1024]{3,2,1,0:T(8,128)(2,1)} %shard_map.64) | data formatting | bytes 524288

commit v3 on v2

v3 whole, which is shorter than its diff:
```python
import functools

import jax
import jax.numpy as jnp
from jax import lax
from jax.experimental import pallas as pl
from jax.experimental.pallas import tpu as pltpu
from jax.sharding import PartitionSpec as P

HEADS = 16
FRAMES = 8
NX, NY, NZ = 4, 8, 4
MESH = pl.DeviceIdType.MESH
F32 = jnp.float32
BF16 = jnp.bfloat16

NAMES = ["own0", "own1"]
NAMES += [f"z{_k}{_s}{_h}" for _k in "pmf" for _s in range(2) for _h in range(2)]
NAMES += [f"share{_s}{_h}" for _s in range(2, 8) for _h in range(2)]
NAMES += ["pair0", "pair1", "y1p", "y1m", "y2p", "y2m", "y3p", "y3m", "y4p", "y4m"]
NAMES += [f"x{_k}{_d}" for _k in "pmf" for _d in range(NY)]
NAMES += [f"slab{_k}" for _k in range(NX)]
NAMES += ["ox1", "ox2", "ox3"]
NAMES += [f"ring{_k}{_s}{_d}" for _k in "pm" for _s in range(1, 5) for _d in range(NX)]
NAMES += [f"rows{_k}" for _k in range(NY)]
INDEX = {name: at for at, name in enumerate(NAMES)}


def kernel(tok_in, wkv_in, wq_in, wo_in, slots_ref, counts_ref, out_ref,
           tok, wkv, wq, wo, kv, qs, att, picked, hits, scores, send, recv, near):
    b = lax.axis_index("blk")
    w = lax.axis_index("win")
    core, zh = lax.rem(b, 2), b // 2
    zl, y, x = lax.rem(w, 2), lax.rem(w // 2, NY), w // (2 * NY)

    def at_z(d):
        return (lax.rem(zh + d, NZ) * 2, w)

    def at_xy(dx, dy, zz):
        return (b, (lax.rem(x + dx, NX) * NY + lax.rem(y + dy, NY)) * 2 + zz)

    sib = (b + 1 - 2 * core, w)
    zp, zm = at_z(1), at_z(NZ - 1)
    pair = at_xy(0, 0, 1 - zl)
    xp, xm, x2 = at_xy(1, 0, zl), at_xy(NX - 1, 0, zl), at_xy(2, 0, zl)
    y1p, y1m = at_xy(0, 1, zl), at_xy(0, NY - 1, zl)
    y2p, y2m = at_xy(0, 2, zl), at_xy(0, NY - 2, zl)

    started = {0: [], 1: []}

    def descriptor(name, src, dst, device):
        return pltpu.make_async_remote_copy(
            src_ref=src, dst_ref=dst, send_sem=send.at[INDEX[name]], recv_sem=recv.at[INDEX[name]],
            device_id=device, device_id_type=MESH,
        )

    def move(who, name, src, dst, device):
        descriptor(name, src, dst, device).start()
        size = 1
        for n in dst.shape:
            size *= n
        started[who].append((name, size // 1024))

    def got(name, dst):
        descriptor(name, dst, dst, sib).wait_recv()

    def enter(devices):
        barrier = pltpu.get_barrier_semaphore()
        for device in devices:
            pl.semaphore_signal(barrier, inc=1, device_id=device, device_id_type=MESH)
        pl.semaphore_wait(barrier, len(devices))

    def sent(who):
        for name, rows in started[who]:
            part = tok.at[0, pl.ds(0, rows)] if rows <= 128 else wq.at[0, pl.ds(0, rows)]
            descriptor(name, part, part, sib).wait_send()

    load_tok = pltpu.make_async_copy(tok_in.at[0, 0], tok.at[core], near.at[0])
    load_tok.start()
    load_kv = pltpu.make_async_copy(wkv_in, wkv, near.at[1])
    load_kv.start()

    before, after, across = lax.rem(zh + NZ - 1, NZ) * 2, lax.rem(zh + 1, NZ) * 2, lax.rem(zh + 2, NZ) * 2
    frames = [2 * zh, 2 * zh + 1, before, after, before + 1, after + 1, across, across + 1]
    wanted = slots_ref[pl.ds(b, 1), 0, :]

    def part(slot, h):
        return tok.at[slot, pl.ds(64 * h, 64)]

    def spread(s):
        for k, h in (("p", 0), ("m", 1), ("p", 1), ("m", 0)):
            src = tok_in.at[0, 0, pl.ds(64 * h, 64)] if s == 0 else part(1, h)
            move(0, f"z{k}{s}{h}", src, part((2 if k == "p" else 3) + 2 * s, h), zp if k == "p" else zm)

    def share(slot, h):
        move(0, f"share{slot}{h}", part(slot, h), part(slot, h), sib)

    def z_pass(s):
        low, high = 2 + 2 * s, 3 + 2 * s
        got(f"zp{s}0", part(low, 0))
        move(0, f"zf{s}0", part(low, 0), part(6 + s, 0), zp)
        got(f"zm{s}1", part(high, 1))
        move(0, f"zf{s}1", part(high, 1), part(6 + s, 1), zm)
        share(low, 0)
        share(high, 1)

    def z_near(s):
        low, high = 2 + 2 * s, 3 + 2 * s
        got(f"zp{s}1", part(low, 1))
        share(low, 1)
        got(f"zm{s}0", part(high, 0))
        share(high, 0)

    def z_far(s):
        got(f"zf{s}0", part(6 + s, 0))
        share(6 + s, 0)
        got(f"zf{s}1", part(6 + s, 1))
        share(6 + s, 1)

    def shared(*slots):
        for slot in slots:
            for h in range(2):
                got(f"share{slot}{h}", part(slot, h))

    def block(buf, k, dx=0, h=None):
        at = lax.rem(y + NY - k, NY) * 32
        if h is None:
            rows = pl.ds(pl.multiple_of(at, 32), 32)
        else:
            rows = pl.ds(pl.multiple_of(at + 16 * h, 16), 16)
        return buf.at[lax.rem(x + dx, NX), rows]

    def slab(k):
        whole = wq.at[lax.rem(x + k, NX)]
        move(1, f"slab{k}", whole, whole, sib)

    def over_x(*ks):
        for k in ks:
            for name, device in (("xp", xp), ("xm", xm)):
                move(1, f"{name}{k}", block(wq, k), block(wq, k), device)

    def pass_x(*ks):
        for k in ks:
            got(f"xp{k}", block(wq, k, NX - 1))
            if k < 4:
                move(1, f"xf{k}", block(wq, k, NX - 1), block(wq, k, NX - 1), xp)
            got(f"xm{k}", block(wq, k, 1))
            if k >= 4:
                move(1, f"xf{k}", block(wq, k, 1), block(wq, k, 1), xm)

    def last_x():
        for k in range(NY):
            got(f"xf{k}", block(wq, k, 2))
        slab(2)

    def y_first():
        for name, device in (("y1p", y1p), ("y1m", y1m), ("y2p", y2p), ("y2m", y2m)):
            move(1, name, block(wq, 0), block(wq, 0), device)

    def y_pass():
        got("y1p", block(wq, 1))
        move(1, "y3p", block(wq, 1), block(wq, 1), y2p)
        got("y1m", block(wq, 7))
        move(1, "y3m", block(wq, 7), block(wq, 7), y2m)
        got("y2p", block(wq, 2))
        move(1, "y4p", block(wq, 2, 0, 0), block(wq, 2, 0, 0), y2p)
        got("y2m", block(wq, 6))
        move(1, "y4m", block(wq, 6, 0, 1), block(wq, 6, 0, 1), y2m)

    def y_last():
        got("y3p", block(wq, 3))
        got("y3m", block(wq, 5))
        got("y4p", block(wq, 4, 0, 0))
        got("y4m", block(wq, 4, 0, 1))

    def ring(step, dx):
        if step < 4 or dx < 2:
            up = block(wo, step - 1, dx)
            move(1, f"ringp{step}{dx}", up, up, y1p)
        if step < 4 or dx >= 2:
            down = block(wo, (NY + 1 - step) % NY, dx)
            move(1, f"ringm{step}{dx}", down, down, y1m)

    def came(step, dx):
        if step < 4 or dx < 2:
            got(f"ringp{step}{dx}", block(wo, step, dx))
        if step < 4 or dx >= 2:
            got(f"ringm{step}{dx}", block(wo, NY - step, dx))

    def ring_pass(step, *dxs):
        for dx in dxs:
            came(step, dx)
            ring(step + 1, dx)

    def rows_of(k):
        at = pl.multiple_of(lax.rem(y + NY - k, NY) * 32, 32)
        return wo.at[:, pl.ds(at, 32)]

    def rows(*ks):
        for k in ks:
            move(1, f"rows{k}", rows_of(k), rows_of(k), sib)

    @pl.when(core == 0)
    def _():
        enter([sib, zp, zm])
        spread(0)
        move(0, "own0", tok_in.at[0, 0], tok.at[0], sib)

    @pl.when(core == 1)
    def _():
        loads = []
        for i, src, buf in ((0, wq_in, wq), (1, wo_in, wo)):
            copy = pltpu.make_async_copy(src, block(buf, 0, 0, zl), near.at[2 + i])
            copy.start()
            loads.append(copy)
        enter([sib, pair, xp, xm, x2, y1p, y1m, y2p, y2m])
        move(1, "own1", tok_in.at[0, 0], tok.at[1], sib)
        move(1, "pair0", wq_in, block(wq, 0, 0, zl), pair)
        move(1, "pair1", wo_in, block(wo, 0, 0, zl), pair)
        for copy in loads:
            copy.wait()

    for j in range(FRAMES):
        token = lax.broadcasted_iota(jnp.int32, (128, 128), 0) + frames[j] * 128
        hits[:, 128 * j:128 * j + 128] = jnp.where(token == wanted, 1.0, 0.0).T.astype(BF16)
    picked[...] = jnp.zeros_like(picked)

    @pl.when(core == 0)
    def _():
        got("own1", tok.at[1])
        spread(1)

    @pl.when(core == 1)
    def _():
        got("pair0", block(wq, 0, 0, 1 - zl))
        y_first()
        over_x(0)
        got("pair1", block(wo, 0, 0, 1 - zl))
        for dx, device in ((1, xp), (3, xm), (2, x2)):
            move(1, f"ox{dx}", block(wo, 0), block(wo, 0), device)
        ring(1, 0)
        got("own0", tok.at[0])

    load_tok.wait()
    load_kv.wait()

    def from_x():
        for dx in (1, 3, 2):
            got(f"ox{dx}", block(wo, 0, (NX - dx) % NX))
            ring(1, (NX - dx) % NX)

    def ring_end():
        for dx in range(NX):
            came(4, dx)

    near_order = (0, 3, 1, 2)
    events = {
        (0, 2): [(z_pass, 0), (z_near, 0)],
        (0, 4): [(z_pass, 1), (z_near, 1)],
        (0, 6): [(z_far, 0)],
        (0, 7): [(z_far, 1)],
        (1, 2): [(y_pass,), (over_x, 1, 7, 2, 6), (from_x,), (rows, 0), (pass_x, 0), (ring_pass, 1) + near_order, (shared, 2)],
        (1, 3): [(y_last,), (over_x, 3, 5, 4), (slab, 0), (shared, 3)],
        (1, 4): [(ring_pass, 2) + near_order, (rows, 1, 7), (pass_x, 1, 7, 2, 6), (ring_pass, 3) + near_order,
                 (rows, 2, 6), (shared, 4)],
        (1, 5): [(pass_x, 3, 5, 4), (slab, 3), (slab, 1), (rows, 3, 5), (shared, 5)],
        (1, 6): [(ring_end,), (rows, 4), (last_x,), (shared, 6)],
        (1, 7): [(shared, 7)],
    }

    @pl.loop(0, FRAMES)
    def _(t):
        for (who, when), calls in events.items():
            @pl.when((core == who) & (t == when))
            def _(calls=calls):
                for call in calls:
                    call[0](*call[1:])

        at = pl.ds(pl.multiple_of(t * 128, 128), 128)
        kv[at, :] = jnp.dot(tok[t], wkv[...], preferred_element_type=F32).astype(BF16)
        picked[...] += jnp.dot(hits[:, at], tok[t], preferred_element_type=F32)

    @pl.when(core == 0)
    def _():
        for k in range(NX):
            got(f"slab{k}", wq.at[lax.rem(x + k, NX)])

    qs[...] = jnp.dot(picked[...].astype(BF16), wq[...].reshape(1024, 1024), preferred_element_type=F32).astype(BF16)

    scale = 64 ** -0.5 * 1.4426950408889634
    lane = lax.broadcasted_iota(jnp.int32, (128, 256), 1)

    def head(h):
        return (lane >= 64 * h) & (lane < 64 * h + 64)

    def score(n):
        rows = qs[:, 256 * n:256 * n + 256]
        zero = jnp.zeros_like(rows)
        stack = jnp.concatenate([jnp.where(head(h), rows, zero) for h in range(4)], axis=0)
        keys = kv[:, 256 * n:256 * n + 256]
        return lax.dot_general(stack, keys, (((1,), (1,)), ((), ())), preferred_element_type=F32)

    groups = HEADS // 4
    scores[0] = score(0)
    for n in range(groups):
        later = score(n + 1) if n + 1 < groups else None
        now = scores[n % 2]
        peak = jnp.max(now, axis=-1, keepdims=True)
        raw = jnp.exp2((now - peak) * scale)
        total = jnp.sum(raw, axis=-1, keepdims=True)
        values = kv[:, 1024 + 256 * n:1280 + 256 * n]
        mixed = jnp.dot(raw.astype(BF16), values, preferred_element_type=F32) / total
        result = mixed[384:]
        for h in range(3):
            result = jnp.where(head(h), mixed[128 * h:128 * h + 128], result)
        att[:, 256 * n:256 * n + 256] = result.astype(BF16)
        if later is not None:
            scores[(n + 1) % 2] = later

    @pl.when(core == 0)
    def _():
        for k in range(NY):
            got(f"rows{k}", rows_of(k))

    live = lax.broadcasted_iota(jnp.int32, (128, 1024), 0) < counts_ref[0, 0]
    result = jnp.dot(att[...], wo[...].reshape(1024, 1024), preferred_element_type=F32)
    out_ref[0, 0] = (result * jnp.where(live, 1.0, 0.0)).astype(BF16)

    for who in range(2):
        pl.when(core == who)(functools.partial(sent, who))


def local(frame_tokens, w_kv, w_q, w_out, slot_tokens, counts):
    hbm = pl.BlockSpec(memory_space=pl.ANY)
    vmem = pl.BlockSpec(memory_space=pltpu.VMEM)
    return pl.pallas_call(
        kernel,
        out_shape=jax.ShapeDtypeStruct((1, 1, 128, 1024), BF16),
        in_specs=[hbm, hbm, hbm, hbm, vmem, pl.BlockSpec(memory_space=pltpu.SMEM)],
        out_specs=vmem,
        scratch_shapes=[
            pltpu.VMEM((8, 128, 1024), BF16),
            pltpu.VMEM((1024, 2048), BF16),
            pltpu.VMEM((NX, 256, 1024), BF16),
            pltpu.VMEM((NX, 256, 1024), BF16),
            pltpu.VMEM((1024, 2048), BF16),
            pltpu.VMEM((128, 1024), BF16),
            pltpu.VMEM((128, 1024), BF16),
            pltpu.VMEM((128, 1024), F32),
            pltpu.VMEM((128, 1024), BF16),
            pltpu.VMEM((2, 512, 1024), F32),
            pltpu.SemaphoreType.DMA((len(NAMES),)),
            pltpu.SemaphoreType.DMA((len(NAMES),)),
            pltpu.SemaphoreType.DMA((4,)),
        ],
        compiler_params=pltpu.CompilerParams(
            collective_id=0, has_side_effects=True, vmem_limit_bytes=56 * 1024 * 1024
        ),
    )(frame_tokens, w_kv, w_q, w_out, slot_tokens, counts)


def solution(mesh):
    placed = (
        P("blk", "win", None, None),
        P(),
        P("win", None),
        P("win", None),
        P(None, "win", None),
        P("blk", "win"),
    )
    return jax.shard_map(
        local, mesh=mesh, in_specs=placed, out_specs=P("blk", "win", None, None), check_vma=False
    )
```

time: 50.5 us -> 48.2 us (0.954)
  the two profiles are of different devices: /device:TPU:73 before, /device:TPU:65 now
where the time goes in v3:
time: 48.2 us; the launch traced here: 48.1 us
  Pallas kernels  45.7 us (95%)
  local copies, waits for them, and re-layouts  1.67 us (3%)
  between operations  0.66 us (1%)
    pallas_call x1, Pallas kernels, local(): pl.pallas_call(kernel, out_shape=jax.ShapeDtypeStruct((1, 1, 128, 1024),...  45.7 us
    unnamed x1, local copies, waits for them, and re-layouts  1.67 us

profile of v3, /device:TPU:65, one launch (start us, length us, event | category | flops | bytes accessed | tf_op | source)
XLA Modules:
  0.0 48.1 jit_solution(12990768112023573841)
XLA Ops:
  0.7 45.7 %shard_map.64 = bf16[1,1,128,1024]{3,2,1,0:T(8,128)(2,1)} custom-call(bf16[1,1,128,1024]{3,2,1,0:T(8,128)(2,1)} %tok_in.1, bf16[1024,2048]{1,0:T(8,128)(2,1)} %wkv_in.1, bf16[16,1024]{1,0:T(8,128)(2,1)} %wq_in.1, bf16[16,1024]{1,0:T(8,128)(2,1)} %wo_in.1, s32[8,1,128]{2,1,0:T(1,128)} %slots_ref.1, s32[1,1]{1,0:T(1,128)S(6)} %copy.8.counts_ref), custom_call_target="tpu_custom_call" | custom-call | tf_op jit(solution)/shard_map/pallas_call | solution.py:336
  46.4 1.7 %copy.9 = bf16[1,1,128,1024]{3,2,1,0:T(8,128)(2,1)} copy(bf16[1,1,128,1024]{3,2,1,0:T(8,128)(2,1)} %shard_map.64) | data formatting | bytes 524288

commit v4 on v3

--- a/solution.py
+++ b/solution.py
@@ -27,7 +27,7 @@
 
 
 def kernel(tok_in, wkv_in, wq_in, wo_in, slots_ref, counts_ref, out_ref,
-           tok, wkv, wq, wo, kv, qs, att, picked, hits, scores, send, recv, near):
+           tok, wkv, wq, wo, kv, qs, att, picked, hits, scores, send, recv, near, hello):
     b = lax.axis_index("blk")
     w = lax.axis_index("win")
     core, zh = lax.rem(b, 2), b // 2
@@ -59,16 +59,19 @@
         size = 1
         for n in dst.shape:
             size *= n
-        started[who].append((name, size // 1024))
+        if (name, size // 1024) not in started[who]:
+            started[who].append((name, size // 1024))
 
     def got(name, dst):
         descriptor(name, dst, dst, sib).wait_recv()
 
-    def enter(devices):
+    def announce(devices):
         barrier = pltpu.get_barrier_semaphore()
         for device in devices:
             pl.semaphore_signal(barrier, inc=1, device_id=device, device_id_type=MESH)
-        pl.semaphore_wait(barrier, len(devices))
+
+    def arrive(count):
+        pl.semaphore_wait(pltpu.get_barrier_semaphore(), count)
 
     def sent(who):
         for name, rows in started[who]:
@@ -200,9 +203,17 @@
         for k in ks:
             move(1, f"rows{k}", rows_of(k), rows_of(k), sib)
 
+    def give_own():
+        pl.semaphore_wait(hello, 1)
+        descriptor("own1", tok_in.at[0, 0], tok.at[1], sib).start()
+
+    started[1].append(("own1", 128))
+
     @pl.when(core == 0)
     def _():
-        enter([sib, zp, zm])
+        announce([zp, zm])
+        arrive(3)
+        pl.semaphore_signal(hello, inc=1, device_id=sib, device_id_type=MESH)
         spread(0)
         move(0, "own0", tok_in.at[0, 0], tok.at[0], sib)
 
@@ -213,8 +224,10 @@
             copy = pltpu.make_async_copy(src, block(buf, 0, 0, zl), near.at[2 + i])
             copy.start()
             loads.append(copy)
-        enter([sib, pair, xp, xm, x2, y1p, y1m, y2p, y2m])
-        move(1, "own1", tok_in.at[0, 0], tok.at[1], sib)
+        across_xy = [pair, xp, xm, x2, y1p, y1m, y2p, y2m]
+        announce([sib] + across_xy)
+        pl.when(zh >= NZ // 2)(give_own)
+        arrive(len(across_xy))
         move(1, "pair0", wq_in, block(wq, 0, 0, zl), pair)
         move(1, "pair1", wo_in, block(wo, 0, 0, zl), pair)
         for copy in loads:
@@ -239,6 +252,7 @@
         for dx, device in ((1, xp), (3, xm), (2, x2)):
             move(1, f"ox{dx}", block(wo, 0), block(wo, 0), device)
         ring(1, 0)
+        pl.when(zh < NZ // 2)(give_own)
         got("own0", tok.at[0])
 
     load_tok.wait()
@@ -254,24 +268,37 @@
             came(4, dx)
 
     near_order = (0, 3, 1, 2)
-    events = {
-        (0, 2): [(z_pass, 0), (z_near, 0)],
-        (0, 4): [(z_pass, 1), (z_near, 1)],
-        (0, 6): [(z_far, 0)],
-        (0, 7): [(z_far, 1)],
-        (1, 2): [(y_pass,), (over_x, 1, 7, 2, 6), (from_x,), (rows, 0), (pass_x, 0), (ring_pass, 1) + near_order, (shared, 2)],
-        (1, 3): [(y_last,), (over_x, 3, 5, 4), (slab, 0), (shared, 3)],
-        (1, 4): [(ring_pass, 2) + near_order, (rows, 1, 7), (pass_x, 1, 7, 2, 6), (ring_pass, 3) + near_order,
-                 (rows, 2, 6), (shared, 4)],
-        (1, 5): [(pass_x, 3, 5, 4), (slab, 3), (slab, 1), (rows, 3, 5), (shared, 5)],
-        (1, 6): [(ring_end,), (rows, 4), (last_x,), (shared, 6)],
-        (1, 7): [(shared, 7)],
-    }
+    early, late = zh < NZ // 2, zh >= NZ // 2
+    first = core == 0
+    by_y = [(y_pass,), (over_x, 1, 7, 2, 6), (from_x,), (rows, 0), (pass_x, 0), (ring_pass, 1) + near_order]
+    by_y_end = [(y_last,), (over_x, 3, 5, 4), (slab, 0)]
+    middle = [(ring_pass, 2) + near_order, (rows, 1, 7), (pass_x, 1, 7, 2, 6), (ring_pass, 3) + near_order, (rows, 2, 6)]
+    by_x_end = [(pass_x, 3, 5, 4), (slab, 3), (slab, 1), (rows, 3, 5)]
+    finish = [(ring_end,), (rows, 4), (last_x,)]
+    events = [
+        (first, 2, [(z_pass, 0), (z_near, 0)]),
+        (first, 4, [(z_pass, 1), (z_near, 1)]),
+        (first, 6, [(z_far, 0)]),
+        (first, 7, [(z_far, 1)]),
+        (~first, 2, by_y),
+        (~first & early, 2, by_y_end + [(ring_pass, 2) + near_order, (rows, 1, 7)]),
+        (~first, 2, [(shared, 2)]),
+        (~first & late, 3, by_y_end),
+        (~first & early, 3, [(pass_x, 1, 7, 2, 6)]),
+        (~first, 3, [(shared, 3)]),
+        (~first & late, 4, middle),
+        (~first & early, 4, [(ring_pass, 3) + near_order, (rows, 2, 6)] + by_x_end),
+        (~first, 4, [(shared, 4)]),
+        (~first & late, 5, by_x_end),
+        (~first, 5, [(shared, 5)]),
+        (~first, 6, finish + [(shared, 6)]),
+        (~first, 7, [(shared, 7)]),
+    ]
 
     @pl.loop(0, FRAMES)
     def _(t):
-        for (who, when), calls in events.items():
-            @pl.when((core == who) & (t == when))
+        for who, when, calls in events:
+            @pl.when(who & (t == when))
             def _(calls=calls):
                 for call in calls:
                     call[0](*call[1:])
@@ -352,6 +379,7 @@
             pltpu.SemaphoreType.DMA((len(NAMES),)),
             pltpu.SemaphoreType.DMA((len(NAMES),)),
             pltpu.SemaphoreType.DMA((4,)),
+            pltpu.SemaphoreType.REGULAR,
         ],
         compiler_params=pltpu.CompilerParams(
             collective_id=0, has_side_effects=True, vmem_limit_bytes=56 * 1024 * 1024

time: 48.2 us -> 45.5 us (0.944)
  the two profiles are of different devices: /device:TPU:65 before, /device:TPU:1 now
where the time goes in v4:
time: 45.5 us; the launch traced here: 45.4 us
  Pallas kernels  43 us (95%)
  local copies, waits for them, and re-layouts  1.67 us (4%)
  between operations  0.66 us (1%)
    pallas_call x1, Pallas kernels, local(): pl.pallas_call(kernel, out_shape=jax.ShapeDtypeStruct((1, 1, 128, 1024),...  43 us
    unnamed x1, local copies, waits for them, and re-layouts  1.67 us

profile of v4, /device:TPU:1, one launch (start us, length us, event | category | flops | bytes accessed | tf_op | source)
XLA Modules:
  0.0 45.4 jit_solution(11295076712080053888)
XLA Ops:
  0.7 43.0 %shard_map.64 = bf16[1,1,128,1024]{3,2,1,0:T(8,128)(2,1)} custom-call(bf16[1,1,128,1024]{3,2,1,0:T(8,128)(2,1)} %tok_in.1, bf16[1024,2048]{1,0:T(8,128)(2,1)} %wkv_in.1, bf16[16,1024]{1,0:T(8,128)(2,1)} %wq_in.1, bf16[16,1024]{1,0:T(8,128)(2,1)} %wo_in.1, s32[8,1,128]{2,1,0:T(1,128)} %slots_ref.1, s32[1,1]{1,0:T(1,128)S(6)} %copy.8.counts_ref), custom_call_target="tpu_custom_call" | custom-call | tf_op jit(solution)/shard_map/pallas_call | solution.py:363
  43.7 1.7 %copy.9 = bf16[1,1,128,1024]{3,2,1,0:T(8,128)(2,1)} copy(bf16[1,1,128,1024]{3,2,1,0:T(8,128)(2,1)} %shard_map.64) | data formatting | bytes 524288

commit v5 on v4

--- a/solution.py
+++ b/solution.py
@@ -23,7 +23,20 @@
 NAMES += ["ox1", "ox2", "ox3"]
 NAMES += [f"ring{_k}{_s}{_d}" for _k in "pm" for _s in range(1, 5) for _d in range(NX)]
 NAMES += [f"rows{_k}" for _k in range(NY)]
-INDEX = {name: at for at, name in enumerate(NAMES)}
+KINDS = ("own", "z", "share", "pair", "y", "x", "slab", "ox", "ring", "rows")
+
+
+def kind_of(name):
+    for kind in sorted(KINDS, key=len, reverse=True):
+        if name.startswith(kind):
+            return KINDS.index(kind)
+
+
+INDEX = {}
+for _name in NAMES:
+    _key = _name[:2] if _name[:2] == "xf" else _name[:4] if _name[:4] in ("rows", "slab") else _name
+    INDEX[_name] = INDEX.setdefault(_key, len(set(INDEX.values())))
+SLOTS = max(INDEX.values()) + 1
 
 
 def kernel(tok_in, wkv_in, wq_in, wo_in, slots_ref, counts_ref, out_ref,
@@ -46,21 +59,14 @@
     y1p, y1m = at_xy(0, 1, zl), at_xy(0, NY - 1, zl)
     y2p, y2m = at_xy(0, 2, zl), at_xy(0, NY - 2, zl)
 
-    started = {0: [], 1: []}
-
     def descriptor(name, src, dst, device):
         return pltpu.make_async_remote_copy(
-            src_ref=src, dst_ref=dst, send_sem=send.at[INDEX[name]], recv_sem=recv.at[INDEX[name]],
+            src_ref=src, dst_ref=dst, send_sem=send.at[kind_of(name)], recv_sem=recv.at[INDEX[name]],
             device_id=device, device_id_type=MESH,
         )
 
     def move(who, name, src, dst, device):
         descriptor(name, src, dst, device).start()
-        size = 1
-        for n in dst.shape:
-            size *= n
-        if (name, size // 1024) not in started[who]:
-            started[who].append((name, size // 1024))
 
     def got(name, dst):
         descriptor(name, dst, dst, sib).wait_recv()
@@ -74,9 +80,16 @@
         pl.semaphore_wait(pltpu.get_barrier_semaphore(), count)
 
     def sent(who):
-        for name, rows in started[who]:
-            part = tok.at[0, pl.ds(0, rows)] if rows <= 128 else wq.at[0, pl.ds(0, rows)]
+        kinds = (("own0", tok.at[0]), ("zp00", tok.at[pl.ds(0, 6)]), ("share20", tok.at[pl.ds(0, 6)])) if who == 0 else (
+            ("own1", tok.at[0]), ("pair0", wq.at[0, pl.ds(0, 32)]), ("y1p", wq.at[0, pl.ds(0, 224)]),
+            ("xp0", wq.at[pl.ds(0, 3)]), ("slab0", wq), ("ox1", wq.at[0, pl.ds(0, 96)]),
+            ("ringp10", tok.at[pl.ds(0, 7)]), ("rows0", wo))
+        for name, part in kinds:
             descriptor(name, part, part, sib).wait_send()
+
+    across_xy = [pair, xp, xm, x2, y1p, y1m, y2p, y2m]
+    pl.when(core == 0)(lambda: announce([zp, zm]))
+    pl.when(core == 1)(lambda: announce([sib] + across_xy))
 
     load_tok = pltpu.make_async_copy(tok_in.at[0, 0], tok.at[core], near.at[0])
     load_tok.start()
@@ -152,8 +165,7 @@
                 move(1, f"xf{k}", block(wq, k, 1), block(wq, k, 1), xm)
 
     def last_x():
-        for k in range(NY):
-            got(f"xf{k}", block(wq, k, 2))
+        got("xf0", wq.at[lax.rem(x + 2, NX)])
         slab(2)
 
     def y_first():
@@ -207,11 +219,8 @@
         pl.semaphore_wait(hello, 1)
         descriptor("own1", tok_in.at[0, 0], tok.at[1], sib).start()
 
-    started[1].append(("own1", 128))
-
     @pl.when(core == 0)
     def _():
-        announce([zp, zm])
         arrive(3)
         pl.semaphore_signal(hello, inc=1, device_id=sib, device_id_type=MESH)
         spread(0)
@@ -224,8 +233,6 @@
             copy = pltpu.make_async_copy(src, block(buf, 0, 0, zl), near.at[2 + i])
             copy.start()
             loads.append(copy)
-        across_xy = [pair, xp, xm, x2, y1p, y1m, y2p, y2m]
-        announce([sib] + across_xy)
         pl.when(zh >= NZ // 2)(give_own)
         arrive(len(across_xy))
         move(1, "pair0", wq_in, block(wq, 0, 0, zl), pair)
@@ -309,8 +316,7 @@
 
     @pl.when(core == 0)
     def _():
-        for k in range(NX):
-            got(f"slab{k}", wq.at[lax.rem(x + k, NX)])
+        got("slab0", wq)
 
     qs[...] = jnp.dot(picked[...].astype(BF16), wq[...].reshape(1024, 1024), preferred_element_type=F32).astype(BF16)
 
@@ -346,8 +352,7 @@
 
     @pl.when(core == 0)
     def _():
-        for k in range(NY):
-            got(f"rows{k}", rows_of(k))
+        got("rows0", wo)
 
     live = lax.broadcasted_iota(jnp.int32, (128, 1024), 0) < counts_ref[0, 0]
     result = jnp.dot(att[...], wo[...].reshape(1024, 1024), preferred_element_type=F32)
@@ -376,8 +381,8 @@
             pltpu.VMEM((128, 1024), F32),
             pltpu.VMEM((128, 1024), BF16),
             pltpu.VMEM((2, 512, 1024), F32),
-            pltpu.SemaphoreType.DMA((len(NAMES),)),
-            pltpu.SemaphoreType.DMA((len(NAMES),)),
+            pltpu.SemaphoreType.DMA((len(KINDS),)),
+            pltpu.SemaphoreType.DMA((SLOTS,)),
             pltpu.SemaphoreType.DMA((4,)),
             pltpu.SemaphoreType.REGULAR,
         ],

time: 45.5 us -> 44.4 us (0.976)
  Pallas kernels: 43 us -> 41.9 us
    pallas_call x1, Pallas kernels: 43 us -> 41.9 us  [local(): pl.pallas_call(kernel, out_shape=jax.ShapeDtypeStruct((1, 1, 128, 1024),...]
where the time goes in v5:
time: 44.4 us; the launch traced here: 44.2 us
  Pallas kernels  41.9 us (94%)
  local copies, waits for them, and re-layouts  1.67 us (4%)
  between operations  0.66 us (1%)
    pallas_call x1, Pallas kernels, local(): pl.pallas_call(kernel, out_shape=jax.ShapeDtypeStruct((1, 1, 128, 1024),...  41.9 us
    unnamed x1, local copies, waits for them, and re-layouts  1.67 us

profile of v5, /device:TPU:1, one launch (start us, length us, event | category | flops | bytes accessed | tf_op | source)
XLA Modules:
  0.0 44.2 jit_solution(9535481792477727715)
XLA Ops:
  0.7 41.9 %shard_map.64 = bf16[1,1,128,1024]{3,2,1,0:T(8,128)(2,1)} custom-call(bf16[1,1,128,1024]{3,2,1,0:T(8,128)(2,1)} %tok_in.1, bf16[1024,2048]{1,0:T(8,128)(2,1)} %wkv_in.1, bf16[16,1024]{1,0:T(8,128)(2,1)} %wq_in.1, bf16[16,1024]{1,0:T(8,128)(2,1)} %wo_in.1, s32[8,1,128]{2,1,0:T(1,128)} %slots_ref.1, s32[1,1]{1,0:T(1,128)S(6)} %copy.8.counts_ref), custom_call_target="tpu_custom_call" | custom-call | tf_op jit(solution)/shard_map/pallas_call | solution.py:368
  42.5 1.7 %copy.9 = bf16[1,1,128,1024]{3,2,1,0:T(8,128)(2,1)} copy(bf16[1,1,128,1024]{3,2,1,0:T(8,128)(2,1)} %shard_map.64) | data formatting | bytes 524288

commit v6 on v5

--- a/solution.py
+++ b/solution.py
@@ -34,7 +34,7 @@
 
 INDEX = {}
 for _name in NAMES:
-    _key = _name[:2] if _name[:2] == "xf" else _name[:4] if _name[:4] in ("rows", "slab") else _name
+    _key = _name[:2] if _name[:2] == "xf" else _name[:6] if _name[:5] == "share" else _name[:4] if _name[:4] in ("rows", "slab") else _name
     INDEX[_name] = INDEX.setdefault(_key, len(set(INDEX.values())))
 SLOTS = max(INDEX.values()) + 1
 
@@ -135,8 +135,7 @@
 
     def shared(*slots):
         for slot in slots:
-            for h in range(2):
-                got(f"share{slot}{h}", part(slot, h))
+            got(f"share{slot}0", tok.at[slot])
 
     def block(buf, k, dx=0, h=None):
         at = lax.rem(y + NY - k, NY) * 32
@@ -260,7 +259,6 @@
             move(1, f"ox{dx}", block(wo, 0), block(wo, 0), device)
         ring(1, 0)
         pl.when(zh < NZ // 2)(give_own)
-        got("own0", tok.at[0])
 
     load_tok.wait()
     load_kv.wait()
@@ -275,11 +273,10 @@
             came(4, dx)
 
     near_order = (0, 3, 1, 2)
-    early, late = zh < NZ // 2, zh >= NZ // 2
     first = core == 0
-    by_y = [(y_pass,), (over_x, 1, 7, 2, 6), (from_x,), (rows, 0), (pass_x, 0), (ring_pass, 1) + near_order]
+    by_y = [(y_pass,), (over_x, 1, 7, 2, 6), (from_x,), (rows, 0)]
+    by_y_next = [(pass_x, 0), (ring_pass, 1) + near_order]
     by_y_end = [(y_last,), (over_x, 3, 5, 4), (slab, 0)]
-    middle = [(ring_pass, 2) + near_order, (rows, 1, 7), (pass_x, 1, 7, 2, 6), (ring_pass, 3) + near_order, (rows, 2, 6)]
     by_x_end = [(pass_x, 3, 5, 4), (slab, 3), (slab, 1), (rows, 3, 5)]
     finish = [(ring_end,), (rows, 4), (last_x,)]
     events = [
@@ -287,16 +284,15 @@
         (first, 4, [(z_pass, 1), (z_near, 1)]),
         (first, 6, [(z_far, 0)]),
         (first, 7, [(z_far, 1)]),
-        (~first, 2, by_y),
-        (~first & early, 2, by_y_end + [(ring_pass, 2) + near_order, (rows, 1, 7)]),
+        (~first, 0, by_y),
+        (~first, 0, [(got, "own0", tok.at[0])]),
+        (~first, 1, by_y_next),
+        (~first, 2, by_y_end + [(ring_pass, 2) + near_order, (rows, 1, 7)]),
         (~first, 2, [(shared, 2)]),
-        (~first & late, 3, by_y_end),
-        (~first & early, 3, [(pass_x, 1, 7, 2, 6)]),
+        (~first, 3, [(pass_x, 1, 7, 2, 6)]),
         (~first, 3, [(shared, 3)]),
-        (~first & late, 4, middle),
-        (~first & early, 4, [(ring_pass, 3) + near_order, (rows, 2, 6)] + by_x_end),
+        (~first, 4, [(ring_pass, 3) + near_order, (rows, 2, 6)] + by_x_end),
         (~first, 4, [(shared, 4)]),
-        (~first & late, 5, by_x_end),
         (~first, 5, [(shared, 5)]),
         (~first, 6, finish + [(shared, 6)]),
         (~first, 7, [(shared, 7)]),

time: 44.4 us -> 42.5 us (0.957)
  the two profiles are of different devices: /device:TPU:1 before, /device:TPU:33 now
where the time goes in v6:
time: 42.5 us; the launch traced here: 42.3 us
  Pallas kernels  40 us (94%)
  local copies, waits for them, and re-layouts  1.67 us (4%)
  between operations  0.66 us (2%)
    pallas_call x1, Pallas kernels, local(): pl.pallas_call(kernel, out_shape=jax.ShapeDtypeStruct((1, 1, 128, 1024),...  40 us
    unnamed x1, local copies, waits for them, and re-layouts  1.67 us

profile of v6, /device:TPU:33, one launch (start us, length us, event | category | flops | bytes accessed | tf_op | source)
XLA Modules:
  0.0 42.3 jit_solution(13125414106801639936)
XLA Ops:
  0.7 40.0 %shard_map.64 = bf16[1,1,128,1024]{3,2,1,0:T(8,128)(2,1)} custom-call(bf16[1,1,128,1024]{3,2,1,0:T(8,128)(2,1)} %tok_in.1, bf16[1024,2048]{1,0:T(8,128)(2,1)} %wkv_in.1, bf16[16,1024]{1,0:T(8,128)(2,1)} %wq_in.1, bf16[16,1024]{1,0:T(8,128)(2,1)} %wo_in.1, s32[8,1,128]{2,1,0:T(1,128)} %slots_ref.1, s32[1,1]{1,0:T(1,128)S(6)} %copy.8.counts_ref), custom_call_target="tpu_custom_call" | custom-call | tf_op jit(solution)/shard_map/pallas_call | solution.py:364
  40.6 1.7 %copy.9 = bf16[1,1,128,1024]{3,2,1,0:T(8,128)(2,1)} copy(bf16[1,1,128,1024]{3,2,1,0:T(8,128)(2,1)} %shard_map.64) | data formatting | bytes 524288

commit v7 on v6

--- a/solution.py
+++ b/solution.py
@@ -284,9 +284,7 @@
         (first, 4, [(z_pass, 1), (z_near, 1)]),
         (first, 6, [(z_far, 0)]),
         (first, 7, [(z_far, 1)]),
-        (~first, 0, by_y),
-        (~first, 0, [(got, "own0", tok.at[0])]),
-        (~first, 1, by_y_next),
+        (~first, 2, by_y_next),
         (~first, 2, by_y_end + [(ring_pass, 2) + near_order, (rows, 1, 7)]),
         (~first, 2, [(shared, 2)]),
         (~first, 3, [(pass_x, 1, 7, 2, 6)]),
@@ -298,7 +296,17 @@
         (~first, 7, [(shared, 7)]),
     ]
 
-    @pl.loop(0, FRAMES)
+    @pl.when(~first)
+    def _():
+        for call in by_y:
+            call[0](*call[1:])
+        got("own0", tok.at[0])
+
+    pair_rows = tok[0:2].reshape(256, 1024)
+    kv[0:256, :] = jnp.dot(pair_rows, wkv[...], preferred_element_type=F32).astype(BF16)
+    picked[...] += jnp.dot(hits[:, 0:256], pair_rows, preferred_element_type=F32)
+
+    @pl.loop(2, FRAMES)
     def _(t):
         for who, when, calls in events:
             @pl.when(who & (t == when))

time: 42.5 us -> 42.5 us (level)
  no operation moved by 1% of the time
where the time goes in v7:
time: 42.5 us; the launch traced here: 42.3 us
  Pallas kernels  40 us (94%)
  local copies, waits for them, and re-layouts  1.67 us (4%)
  between operations  0.66 us (2%)
    pallas_call x1, Pallas kernels, local(): pl.pallas_call(kernel, out_shape=jax.ShapeDtypeStruct((1, 1, 128, 1024),...  40 us
    unnamed x1, local copies, waits for them, and re-layouts  1.67 us

profile of v7, /device:TPU:33, one launch (start us, length us, event | category | flops | bytes accessed | tf_op | source)
XLA Modules:
  0.0 42.3 jit_solution(16025521352775639355)
XLA Ops:
  0.7 40.0 %shard_map.64 = bf16[1,1,128,1024]{3,2,1,0:T(8,128)(2,1)} custom-call(bf16[1,1,128,1024]{3,2,1,0:T(8,128)(2,1)} %tok_in.1, bf16[1024,2048]{1,0:T(8,128)(2,1)} %wkv_in.1, bf16[16,1024]{1,0:T(8,128)(2,1)} %wq_in.1, bf16[16,1024]{1,0:T(8,128)(2,1)} %wo_in.1, s32[8,1,128]{2,1,0:T(1,128)} %slots_ref.1, s32[1,1]{1,0:T(1,128)S(6)} %copy.8.counts_ref), custom_call_target="tpu_custom_call" | custom-call | tf_op jit(solution)/shard_map/pallas_call | solution.py:372
  40.6 1.7 %copy.9 = bf16[1,1,128,1024]{3,2,1,0:T(8,128)(2,1)} copy(bf16[1,1,128,1024]{3,2,1,0:T(8,128)(2,1)} %shard_map.64) | data formatting | bytes 524288
